TPU v7x, 512 devices: a whole 4x8x8 slice. The times are simulated.
512 devices in a mesh: dp: 32 (over z, y_lo, core), tensor: 16 (over y_hi, x).
Axes of the slice: x: 4, y: 8 (y_hi: 4, y_lo: 2; y = y_hi * 2 + y_lo), z: 8, core: 2. Of those that a mesh axis runs over, the one named last changes fastest.
Arguments:
- tokens: bfloat16 [3072, 8192], P('tensor', 'dp'), may hold values from -6 to 6
- w_gate: bfloat16 [8192, 26624], P('dp', 'tensor'), may hold values from -0.0625 to 0.0625
- gate_pre: bfloat16 [3072, 26624], P('dp', 'tensor'), may hold values from -8 to 8
- up_act: bfloat16 [3072, 26624], P('dp', 'tensor'), may hold values from -6 to 6
- d_hidden: bfloat16 [3072, 26624], P('dp', 'tensor'), may hold values from -6 to 6
- block_mask: int32 [64, 208, 8], P('dp', 'tensor'), may hold values 0 or 1
- lang_ids: int32 [3072], P('tensor'), may hold values from 0 to 7
Outputs:
- input_grad: bfloat16 [3072, 8192], P('tensor', 'dp')
- weight_grad: float32 [8192, 26624], P('dp', 'tensor')
All inputs are finite; a program needn't handle non-finite values. No bound on the sum of `block_mask` on one device may be relied on, other than what follows from the above.
Results may differ from a plain program's by a relative error of at most 0.0049.
Values may be sent and summed in bfloat16 or wider, within the bound.
A program may use at most 128 MiB of HBM per device.

v0:
```python
import jax
import jax.numpy as jnp
from jax import lax
from jax.sharding import PartitionSpec as P


def lookup_masks(language_ids, block_mask):
    language_count = block_mask.shape[2]
    onehot = (language_ids[:, None] == jnp.arange(language_count, dtype=jnp.int32)[None, :]).astype(
        jnp.bfloat16
    )
    table = block_mask.astype(jnp.bfloat16)
    return jnp.einsum("nl,kjl->nkj", onehot, table, preferred_element_type=jnp.float32).astype(
        jnp.bfloat16
    )


def input_rows_of(gradients, mask_rows, w_blocks):
    row_count = gradients.shape[0]
    row_blocks, block_size, col_blocks, _ = w_blocks.shape
    shaped = gradients.reshape(row_count, col_blocks, block_size)

    def input_one_rowblock(block_index):
        mask_part = lax.dynamic_index_in_dim(mask_rows, block_index, 1, keepdims=False)
        scaled = shaped * mask_part[:, :, None]
        w_part = lax.dynamic_index_in_dim(w_blocks, block_index, 0, keepdims=False)
        return jnp.einsum("njf,djf->nd", scaled, w_part, preferred_element_type=jnp.float32)

    parts = lax.map(input_one_rowblock, jnp.arange(row_blocks, dtype=jnp.int32))
    return jnp.transpose(parts, (1, 0, 2)).reshape(row_count, row_blocks * block_size)


def weight_product(row_data, gradients, mask_rows):
    row_count = row_data.shape[0]
    row_blocks = mask_rows.shape[1]
    col_blocks = mask_rows.shape[2]
    block_size = row_data.shape[1] // row_blocks
    shaped = gradients.reshape(row_count, col_blocks, block_size)

    def weight_one_rowblock(block_index):
        mask_part = lax.dynamic_index_in_dim(mask_rows, block_index, 1, keepdims=False)
        scaled = shaped * mask_part[:, :, None]
        data_part = lax.dynamic_slice_in_dim(row_data, block_index * block_size, block_size, 1)
        return jnp.einsum("nd,njf->djf", data_part, scaled, preferred_element_type=jnp.float32)

    parts = lax.map(weight_one_rowblock, jnp.arange(row_blocks, dtype=jnp.int32))
    return parts.reshape(row_blocks * block_size, col_blocks * block_size)


def local(tokens, w_gate, gate_pre, up_act, d_hidden, block_mask, lang_ids):
    gate_value = gate_pre.astype(jnp.float32)
    sigmoid_gate = jax.nn.sigmoid(gate_value)
    gate_grad = (
        d_hidden.astype(jnp.float32)
        * up_act.astype(jnp.float32)
        * sigmoid_gate
        * (1.0 + gate_value * (1.0 - sigmoid_gate))
    ).astype(jnp.bfloat16)
    all_rows, all_ids = (
        lax.all_gather(tokens, "tensor", axis=0, tiled=True),
        lax.all_gather(lang_ids, "tensor", axis=0, tiled=True),
    )
    token_count = all_rows.shape[0]
    row_blocks = block_mask.shape[0]
    col_blocks = block_mask.shape[1]
    block_size = w_gate.shape[0] // row_blocks
    w_blocks = w_gate.reshape(row_blocks, block_size, col_blocks, block_size)
    arrived = lax.all_gather(gate_grad, "dp", axis=0, tiled=True)
    mask_rows = lookup_masks(all_ids, block_mask)
    weights_sum = weight_product(all_rows, arrived, mask_rows)
    updated = input_rows_of(arrived, mask_rows, w_blocks)
    partial_value = updated
    weights_sum, partial_value = (weights_sum, partial_value)
    input_grad = lax.psum_scatter(partial_value, "tensor", scatter_dimension=0, tiled=True)
    weight_grad = weights_sum / jnp.sqrt(jnp.float32(token_count))
    return (input_grad.astype(jnp.bfloat16), weight_grad)


def solution(mesh):
    placed = (
        P("tensor", "dp"),
        P("dp", "tensor"),
        P("dp", "tensor"),
        P("dp", "tensor"),
        P("dp", "tensor"),
        P("dp", "tensor", None),
        P("tensor"),
    )
    return jax.shard_map(
        local,
        mesh=mesh,
        in_specs=placed,
        out_specs=(P("tensor", "dp"), P("dp", "tensor")),
        check_vma=False,
    )
```

profile of v0, /device:TPU:64, one launch (start us, length us, event | category | flops | bytes accessed | tf_op | source)
XLA Modules:
  0.0 262.1 jit_solution(4391563297279748045)
XLA Ops:
  7.2 0.0 copy-start.1
  7.2 0.0 all-gather.3.cloned.1.call-start
  7.2 2.2 fusion.29
  9.4 0.0 all-gather.3.cloned.1.call-update
  9.4 0.0 all-gather.5.cloned.1.call-start
  9.5 0.7 all-gather.5.cloned.1.call-update
  10.2 0.0 reduce-scatter.2.cloned.1.call-start
  10.3 1.3 dynamic-slice
  12.2 0.9 dynamic-update-slice
  13.1 83.0 %all-reduce = s32[3072]{0:T(1024)S(1)} all-reduce(s32[3072]{0:T(1024)S(1)} %dynamic-update-slice), channel_id=1, replica_groups=mesh['dp'=32,'tensor'=16] {'tensor'}, use_global_device_ids=true, to_apply=%add | all-reduce | flops 3072 | bytes 24576
  96.1 1.7 reshape.33
  97.8 1.1 copy.26
  98.9 0.0 copy-done.1
  98.9 0.2 convolution_convert_fusion
  99.2 0.0 all-gather.3.cloned.1.call-done
  99.2 14.3 %copy.23 = bf16[3072,1664]{0,1:T(8,128)(2,1)} copy(bf16[3072,1664]{1,0:T(8,128)(2,1)} %all-gather.3.cloned.1.call-done) | data formatting | bytes 20447232 | tf_op jit(solution)/shard_map/all_gather | solution.py:68
  113.5 0.0 copy-start
  113.5 14.4 %copy.25 = bf16[3072,13,128]{2,0,1:T(8,128)(2,1)} copy(bf16[3072,13,128]{0,2,1:T(8,128)(2,1)} %bitcast.54) | data formatting | bytes 20447232 | tf_op jit(solution)/shard_map/while | solution.py:29
  127.9 0.0 copy-done
  127.9 25.5 %while.20 = (s32[]{:T(128)}, f32[2,3072,128]{2,1,0:T(8,128)S(1)}, s32[2]{0:T(128)S(1)}, bf16[3072,2,13]{0,2,1:T(8,128)(2,1)S(1)}, bf16[3072,13,128]{2,0,1:T(8,12...) while((s32[]{:T(128)}, f32[2,3072,128]{2,1,0:T(8,128)S(1)}, ...), condition=%wide.region_1.2_spmd, body=%wide.region_0.1_spmd.sunk | while | flops 1313734656 | bytes 12481171 | solution.py:29
  127.9 0.7 dynamic_slice.39
  130.7 9.9 %fusion.43 = f32[2,3072,128]{2,1,0:T(8,128)S(1)} fusion(f32[2,3072,128]{2,1,0:T(8,128)S(1)} %get-tuple-element.204, s32[]{:T(128)} %get-tuple-element.203, bf16[3072,13,128]{2,0,1:T(8,128)(2,1)} %get-tuple-element.216, bf16[3072,13]{0,1:T(8,128)(2,1)S(1)} %dynamic-slice_bitcast_fusion.4, bf16[2,128,13,128]{3,1,2,0:T(8,128)(2,1)} %get-tuple-element.217, ...), kind=kOutput, calls=%fused_computation.4.clone.1 | convolution fusion | flops 1313734656 | bytes 12321284 | tf_op jit(solution)/shard_map/while/body/eval_jaxpr/njf,djf->nd/dot_general | solution.py:27
  140.6 0.7 dynamic_slice.39
  143.4 10.0 %fusion.43 = f32[2,3072,128]{2,1,0:T(8,128)S(1)} fusion(f32[2,3072,128]{2,1,0:T(8,128)S(1)} %get-tuple-element.204, s32[]{:T(128)} %get-tuple-element.203, bf16[3072,13,128]{2,0,1:T(8,128)(2,1)} %get-tuple-element.216, bf16[3072,13]{0,1:T(8,128)(2,1)S(1)} %dynamic-slice_bitcast_fusion.4, bf16[2,128,13,128]{3,1,2,0:T(8,128)(2,1)} %get-tuple-element.217, ...), kind=kOutput, calls=%fused_computation.4.clone.1 | convolution fusion | flops 1313734656 | bytes 12321284 | tf_op jit(solution)/shard_map/while/body/eval_jaxpr/njf,djf->nd/dot_general | solution.py:27
  153.4 2.0 copy_bitcast_fusion
  155.4 0.0 reduce-scatter.2.cloned.1.call-update
  155.4 0.0 all-gather.5.cloned.1.call-done
  155.5 34.0 %while.21 = (s32[]{:T(128)}, f32[2,128,13,128]{3,1,2,0:T(8,128)S(1)}, s32[2]{0:T(128)S(1)}, bf16[3072,256]{1,0:T(8,128)(2,1)}, bf16[3072,2,13]{0,2,1:T(8,128)(2,...) while((s32[]{:T(128)}, ...), condition=%wide.region_4.5_spmd, body=%wide.region_3.4_spmd.sunk | while | flops 1329070080 | bytes 12120785 | solution.py:46
  155.5 0.6 dynamic_slice.42
  158.7 13.8 %fusion.46 = f32[2,128,13,128]{3,1,2,0:T(8,128)S(1)} fusion(f32[2,128,13,128]{3,1,2,0:T(8,128)S(1)} %get-tuple-element.233, s32[]{:T(128)} %get-tuple-element.232, bf16[3072,13,128]{2,0,1:T(8,128)(2,1)} %get-tuple-element.248, bf16[3072,13]{0,1:T(8,128)(2,1)S(1)} %dynamic-slice_bitcast_fusion.5, bf16[3072,256]{1,0:T(8,128)(2,1)} %get-tuple-element.246, ...), kind=kOutput, calls=%fused_computation.13.clone.1 | convolution fusion | flops 1329070080 | bytes 11960836 | tf_op jit(solution)/shard_map/while/body/eval_jaxpr/nd,njf->djf/dot_general | solution.py:44
  172.5 0.6 dynamic_slice.42
  175.7 13.8 %fusion.46 = f32[2,128,13,128]{3,1,2,0:T(8,128)S(1)} fusion(f32[2,128,13,128]{3,1,2,0:T(8,128)S(1)} %get-tuple-element.233, s32[]{:T(128)} %get-tuple-element.232, bf16[3072,13,128]{2,0,1:T(8,128)(2,1)} %get-tuple-element.248, bf16[3072,13]{0,1:T(8,128)(2,1)S(1)} %dynamic-slice_bitcast_fusion.5, bf16[3072,256]{1,0:T(8,128)(2,1)} %get-tuple-element.246, ...), kind=kOutput, calls=%fused_computation.13.clone.1 | convolution fusion | flops 1329070080 | bytes 11960836 | tf_op jit(solution)/shard_map/while/body/eval_jaxpr/nd,njf->djf/dot_general | solution.py:44
  189.4 0.2 broadcast_multiply_fusion
  189.6 1.0 copy.34
  190.6 1.9 copy.41
  192.5 61.5 %reduce-scatter.2.cloned.1.call-done = f32[192,256]{1,0:T(8,128)} async-done(((f32[3072,256]{1,0:T(8,128)}), f32[192,256]{1,0:T(8,128)}) %reduce-scatter.2.cloned.1.call-update) | async-done | bytes 196624 | tf_op jit(solution)/shard_map/reduce_scatter | solution.py:74
  254.0 1.6 convert_element_type.28
  (9 shorter events, 0.1 us)
Async XLA Ops:
  7.2 91.8 %copy-start.1 = (s32[2,13,8]{1,2,0:T(8,128)S(1)}, s32[2,13,8]{1,2,0:T(8,128)}, u32[]{:S(2)}) copy-start(s32[2,13,8]{1,2,0:T(8,128)} %param.16) | copy-start | bytes 2500
  7.2 92.0 %all-gather.3.cloned.1.call-start = ((), (), s32[]{:S(2)}) async-start(), calls=%async_computation.1 | async-start | bytes 10543104 | tf_op jit(solution)/shard_map/all_gather | solution.py:68
  9.4 146.0 %all-gather.5.cloned.1.call-start = ((), (), s32[]{:S(2)}) async-start(), calls=%async_computation.3 | async-start | bytes 1671168 | tf_op jit(solution)/shard_map/all_gather | solution.py:60
  10.2 243.8 %reduce-scatter.2.cloned.1.call-start = ((), (), s32[]{:S(2)}) async-start(), calls=%async_computation.2 | async-start | bytes 3342336 | tf_op jit(solution)/shard_map/reduce_scatter | solution.py:74
  113.5 14.4 %copy-start = (f32[2,3072,128]{2,1,0:T(8,128)S(1)}, f32[2,3072,128]{2,1,0:T(8,128)}, u32[]{:S(2)}) copy-start(f32[2,3072,128]{2,1,0:T(8,128)} %custom-call) | copy-start | bytes 9437188
Sparse Core Ops, SparseCore 0:
  10.2 80.9 all-gather.2
  94.2 60.6 all-gather.4
  159.0 94.9 reduce-scatter.1
where the time goes:
time: 263 us; the launch traced here: 262 us
  blocking collectives  83 us (32%)
  waiting for transfers between devices  62.3 us (24%)
  matrix products  47.6 us (18%)
  local copies, waits for them, and re-layouts  41.2 us (16%)
  between operations  14.5 us (6%)
  loops' own time  9.45 us (4%)
  other arithmetic  3.92 us (1%)
    unnamed x1, blocking collectives  83 us
    reduce_scatter x1, waiting for transfers between devices, local(): lax.psum_scatter(partial_value, 'tensor', scatter_dimension=0, tiled=True)  61.5 us
    dot_general x2, matrix products, weight_one_rowblock(): jnp.einsum('nd,njf->djf', data_part, scaled, preferred_element_type=jnp.f...  27.5 us
    dot_general x2, matrix products, input_one_rowblock(): jnp.einsum('njf,djf->nd', scaled, w_part, preferred_element_type=jnp.floa...  19.9 us
    while x2, local copies, waits for them, and re-layouts, input_rows_of(): parts = lax.map(input_one_rowblock, jnp.arange(row_blocks, dtype=jnp.int32))  15.5 us
    all_gather x1, local copies, waits for them, and re-layouts, local(): arrived = lax.all_gather(gate_grad, 'dp', axis=0, tiled=True)  14.3 us
  transfers between devices with their start and end apart: 3, of which 1 were waited for; matrix products, arithmetic and copies ran while one was open for 34% of the time, Pallas kernels for 0%

commit v1 on v0

--- a/solution.py
+++ b/solution.py
@@ -65,7 +65,8 @@
     col_blocks = block_mask.shape[1]
     block_size = w_gate.shape[0] // row_blocks
     w_blocks = w_gate.reshape(row_blocks, block_size, col_blocks, block_size)
-    arrived = lax.all_gather(gate_grad, "dp", axis=0, tiled=True)
+    repeated = jnp.stack([gate_grad] * lax.axis_size("dp"))
+    arrived = jnp.concatenate(lax.all_to_all(repeated, "dp", 0, 0), axis=0)
     mask_rows = lookup_masks(all_ids, block_mask)
     weights_sum = weight_product(all_rows, arrived, mask_rows)
     updated = input_rows_of(arrived, mask_rows, w_blocks)

time: 263 us -> 471 us (1.79)
  blocking collectives: 83 us -> 269 us
  starting transfers between devices: 0.12 us -> 11.4 us
  waiting for transfers between devices: 62.3 us -> 67.9 us
  local copies, waits for them, and re-layouts: 41.2 us -> 46.4 us
    unnamed x1, blocking collectives: 83 us -> 269 us
    another operation x0 -> x2, local copies, waits for them, and re-layouts: none -> 23.4 us  [the longest x1 18.8 us: input_rows_of(): shaped = gradients.reshape(row_count, col_blocks, block_size)]
    all_gather x1 -> x0, local copies, waits for them, and re-layouts: 14.3 us -> none  [local(): arrived = lax.all_gather(gate_grad, 'dp', axis=0, tiled=True)]
    all_to_all x0 -> x1, starting transfers between devices: none -> 11.3 us  [local(): arrived = jnp.concatenate(lax.all_to_all(repeated, 'dp', 0, 0), axis=0)]
    reduce_scatter x1, waiting for transfers between devices: 61.5 us -> 67.2 us  [local(): lax.psum_scatter(partial_value, 'tensor', scatter_dimension=0, tiled=True)]
  transfers between devices with their start and end apart: 3 -> 3, of which waited for: 1 -> 1; matrix products, arithmetic and copies ran while one was open for 34% -> 19% of each run, Pallas kernels for 0% -> 0%
where the time goes in v1:
time: 471 us; the launch traced here: 470 us
  blocking collectives  269 us (57%)
  waiting for transfers between devices  67.9 us (14%)
  matrix products  47.8 us (10%)
  local copies, waits for them, and re-layouts  46.4 us (10%)
  between operations  14.7 us (3%)
  starting transfers between devices  11.4 us (2%)
  loops' own time  9.45 us (2%)
    unnamed x1, blocking collectives  269 us
    reduce_scatter x1, waiting for transfers between devices, local(): lax.psum_scatter(partial_value, 'tensor', scatter_dimension=0, tiled=True)  67.2 us
    dot_general x2, matrix products, weight_one_rowblock(): jnp.einsum('nd,njf->djf', data_part, scaled, preferred_element_type=jnp.f...  27.6 us
    dot_general x2, matrix products, input_one_rowblock(): jnp.einsum('njf,djf->nd', scaled, w_part, preferred_element_type=jnp.floa...  19.9 us
    another operation x1, local copies, waits for them, and re-layouts, input_rows_of(): shaped = gradients.reshape(row_count, col_blocks, block_size)  18.8 us
    while x2, local copies, waits for them, and re-layouts, input_rows_of(): parts = lax.map(input_one_rowblock, jnp.arange(row_blocks, dtype=jnp.int32))  13.5 us
    all_to_all x1, starting transfers between devices, local(): arrived = jnp.concatenate(lax.all_to_all(repeated, 'dp', 0, 0), axis=0)  11.3 us
  transfers between devices with their start and end apart: 3, of which 1 were waited for; matrix products, arithmetic and copies ran while one was open for 19% of the time, Pallas kernels for 0%

profile of v1, /device:TPU:64, one launch (start us, length us, event | category | flops | bytes accessed | tf_op | source)
XLA Modules:
  0.0 469.7 jit_solution(88831051793891250)
XLA Ops:
  7.2 1.5 fusion.29
  8.6 4.6 stack.2
  13.2 0.0 copy-start.1
  13.2 11.3 %all-to-all-start = ((bf16[32,96,1664]{2,1,0:T(8,128)(2,1)}), bf16[32,96,1664]{2,1,0:T(8,128)(2,1)}, u32[]{:S(2)}, u32[]{:S(2)}) async-start(bf16[32,96,1664]{2,1,0:T(8,128)(2,1)} %stack.2), calls=%async_computation | async-start | bytes 20447232 | tf_op jit(solution)/shard_map/all_to_all | solution.py:69
  24.5 0.0 copy-start.3
  24.6 0.0 copy-start.2
  24.6 0.0 all-gather.2.cloned.1.call-start
  24.6 0.7 all-gather.2.cloned.1.call-update
  25.3 0.0 reduce-scatter.2.cloned.1.call-start
  25.4 0.0 copy-done.1
  25.4 0.6 reshape.30
  26.0 1.1 copy.22
  27.1 1.3 dynamic-slice
  29.0 0.0 copy-done.3
  29.0 0.3 dynamic-update-slice
  29.3 268.8 %all-reduce = s32[3072]{0:T(1024)S(1)} all-reduce(s32[3072]{0:T(1024)S(1)} %dynamic-update-slice), channel_id=1, replica_groups=mesh['dp'=32,'tensor'=16] {'tensor'}, use_global_device_ids=true, to_apply=%add | all-reduce | flops 3072 | bytes 24576
  298.1 0.0 copy-done.2
  298.1 0.2 convolution_convert_fusion
  298.3 0.0 all-to-all-done
  298.3 18.8 %reshape_reshape.4 = bf16[3072,13,128]{2,1,0:T(8,128)(2,1)} reshape(bf16[32,96,1664]{2,1,0:T(8,128)(2,1)} %all-to-all-done) | data formatting | bytes 20447232 | tf_op jit(solution)/shard_map/reshape;reshape | solution.py:21
  317.2 0.0 copy-start
  317.2 12.3 %copy.21 = bf16[3072,13,128]{2,0,1:T(8,128)(2,1)} copy(bf16[3072,13,128]{2,1,0:T(8,128)(2,1)} %reshape_reshape.4) | data formatting | bytes 20447232 | tf_op jit(solution)/shard_map/while | solution.py:29
  329.5 0.0 copy-done
  329.5 25.4 %while.20 = (s32[]{:T(128)}, f32[2,3072,128]{2,1,0:T(8,128)S(1)}, s32[2]{0:T(128)S(1)}, bf16[3072,2,13]{0,2,1:T(8,128)(2,1)S(1)}, bf16[3072,13,128]{2,0,1:T(8,12...) while((s32[]{:T(128)}, f32[2,3072,128]{2,1,0:T(8,128)S(1)}, ...), condition=%wide.region_1.2_spmd, body=%wide.region_0.1_spmd.sunk | while | flops 1313734656 | bytes 12481171 | solution.py:29
  329.5 0.7 dynamic_slice.39
  332.3 9.9 %fusion.43 = f32[2,3072,128]{2,1,0:T(8,128)S(1)} fusion(f32[2,3072,128]{2,1,0:T(8,128)S(1)} %get-tuple-element.204, s32[]{:T(128)} %get-tuple-element.203, bf16[3072,13,128]{2,0,1:T(8,128)(2,1)} %get-tuple-element.216, bf16[3072,13]{0,1:T(8,128)(2,1)S(1)} %dynamic-slice_bitcast_fusion.4, bf16[2,128,13,128]{3,1,2,0:T(8,128)(2,1)} %get-tuple-element.217, ...), kind=kOutput, calls=%fused_computation.4.clone.1 | convolution fusion | flops 1313734656 | bytes 12321284 | tf_op jit(solution)/shard_map/while/body/eval_jaxpr/njf,djf->nd/dot_general | solution.py:27
  342.2 0.7 dynamic_slice.39
  345.0 9.9 %fusion.43 = f32[2,3072,128]{2,1,0:T(8,128)S(1)} fusion(f32[2,3072,128]{2,1,0:T(8,128)S(1)} %get-tuple-element.204, s32[]{:T(128)} %get-tuple-element.203, bf16[3072,13,128]{2,0,1:T(8,128)(2,1)} %get-tuple-element.216, bf16[3072,13]{0,1:T(8,128)(2,1)S(1)} %dynamic-slice_bitcast_fusion.4, bf16[2,128,13,128]{3,1,2,0:T(8,128)(2,1)} %get-tuple-element.217, ...), kind=kOutput, calls=%fused_computation.4.clone.1 | convolution fusion | flops 1313734656 | bytes 12321284 | tf_op jit(solution)/shard_map/while/body/eval_jaxpr/njf,djf->nd/dot_general | solution.py:27
  355.0 1.9 copy_bitcast_fusion
  356.8 0.0 reduce-scatter.2.cloned.1.call-update
  356.9 0.0 all-gather.2.cloned.1.call-done
  356.9 34.1 %while.21 = (s32[]{:T(128)}, f32[2,128,13,128]{3,1,2,0:T(8,128)S(1)}, s32[2]{0:T(128)S(1)}, bf16[3072,256]{1,0:T(8,128)(2,1)}, bf16[3072,2,13]{0,2,1:T(8,128)(2,...) while((s32[]{:T(128)}, ...), condition=%wide.region_4.5_spmd, body=%wide.region_3.4_spmd.sunk | while | flops 1329070080 | bytes 12120785 | solution.py:46
  356.9 0.6 dynamic_slice.42
  360.1 13.8 %fusion.46 = f32[2,128,13,128]{3,1,2,0:T(8,128)S(1)} fusion(f32[2,128,13,128]{3,1,2,0:T(8,128)S(1)} %get-tuple-element.233, s32[]{:T(128)} %get-tuple-element.232, bf16[3072,13,128]{2,0,1:T(8,128)(2,1)} %get-tuple-element.248, bf16[3072,13]{0,1:T(8,128)(2,1)S(1)} %dynamic-slice_bitcast_fusion.5, bf16[3072,256]{1,0:T(8,128)(2,1)} %get-tuple-element.246, ...), kind=kOutput, calls=%fused_computation.13.clone.1 | convolution fusion | flops 1329070080 | bytes 11960836 | tf_op jit(solution)/shard_map/while/body/eval_jaxpr/nd,njf->djf/dot_general | solution.py:44
  373.9 0.6 dynamic_slice.42
  377.1 13.9 %fusion.46 = f32[2,128,13,128]{3,1,2,0:T(8,128)S(1)} fusion(f32[2,128,13,128]{3,1,2,0:T(8,128)S(1)} %get-tuple-element.233, s32[]{:T(128)} %get-tuple-element.232, bf16[3072,13,128]{2,0,1:T(8,128)(2,1)} %get-tuple-element.248, bf16[3072,13]{0,1:T(8,128)(2,1)S(1)} %dynamic-slice_bitcast_fusion.5, bf16[3072,256]{1,0:T(8,128)(2,1)} %get-tuple-element.246, ...), kind=kOutput, calls=%fused_computation.13.clone.1 | convolution fusion | flops 1329070080 | bytes 11960836 | tf_op jit(solution)/shard_map/while/body/eval_jaxpr/nd,njf->djf/dot_general | solution.py:44
  391.0 0.2 broadcast_multiply_fusion
  391.2 1.0 copy.30
  392.2 1.9 copy.37
  394.1 67.2 %reduce-scatter.2.cloned.1.call-done = f32[192,256]{1,0:T(8,128)} async-done(((f32[3072,256]{1,0:T(8,128)}), f32[192,256]{1,0:T(8,128)}) %reduce-scatter.2.cloned.1.call-update) | async-done | bytes 196624 | tf_op jit(solution)/shard_map/reduce_scatter | solution.py:75
  461.3 1.6 convert_element_type.28
  (9 shorter events, 0.1 us)
Async XLA Ops:
  13.2 12.2 %copy-start.1 = (bf16[256,1664]{1,0:T(8,128)(2,1)S(1)}, bf16[256,1664]{1,0:T(8,128)(2,1)}, u32[]{:S(2)}) copy-start(bf16[256,1664]{1,0:T(8,128)(2,1)} %param.12) | copy-start | bytes 2555908
  13.2 285.1 %all-to-all-start = ((bf16[32,96,1664]{2,1,0:T(8,128)(2,1)}), bf16[32,96,1664]{2,1,0:T(8,128)(2,1)}, u32[]{:S(2)}, u32[]{:S(2)}) async-start(bf16[32,96,1664]{2,1,0:T(8,128)(2,1)} %stack.2), calls=%async_computation | async-start | bytes 20447232 | tf_op jit(solution)/shard_map/all_to_all | solution.py:69
  24.5 4.4 copy-start.3
  24.6 273.5 %copy-start.2 = (s32[2,13,8]{1,2,0:T(8,128)S(1)}, s32[2,13,8]{1,2,0:T(8,128)}, u32[]{:S(2)}) copy-start(s32[2,13,8]{1,2,0:T(8,128)} %param.16) | copy-start | bytes 2500
  24.6 332.3 %all-gather.2.cloned.1.call-start = ((), (), s32[]{:S(2)}) async-start(), calls=%async_computation.3 | async-start | bytes 1671168 | tf_op jit(solution)/shard_map/all_gather | solution.py:60
  25.3 436.0 %reduce-scatter.2.cloned.1.call-start = ((), (), s32[]{:S(2)}) async-start(), calls=%async_computation.2 | async-start | bytes 3342336 | tf_op jit(solution)/shard_map/reduce_scatter | solution.py:75
  317.2 12.3 %copy-start = (f32[2,3072,128]{2,1,0:T(8,128)S(1)}, f32[2,3072,128]{2,1,0:T(8,128)}, u32[]{:S(2)}) copy-start(f32[2,3072,128]{2,1,0:T(8,128)} %custom-call) | copy-start | bytes 9437188
Sparse Core Ops, SparseCore 0:
  28.4 73.1 all-gather.1
  357.0 104.2 reduce-scatter.1
